TPU v7x, 256 devices: a whole 4x4x8 slice. The times are simulated.
256 devices in a mesh: seq: 16 (over z, core), ch: 16 (over y, x).
Axes of the slice: x: 4, y: 4, z: 8, core: 2. Of those that a mesh axis runs over, the one named last changes fastest.
Arguments:
- query: bfloat16 [2048, 8192], P('seq', 'ch'), may hold values from -6 to 6
- key: bfloat16 [2048, 8192], P('seq', 'ch'), may hold values from -6 to 6
- value: bfloat16 [2048, 8192], P('seq', 'ch'), may hold values from -6 to 6
- short_taps: float32 [3, 3, 8192], P(None, None, 'ch'), may hold values from -3 to 3
- decay_rate: float32 [16, 8192], P(None, 'ch'), may hold values from 0.00012207031 to 0.05
- residue: float32 [16, 8192], P(None, 'ch'), may hold values from -2 to 2
- skip_gain: float32 [8192], P('ch'), may hold values from -4 to 4
- out_weight: bfloat16 [8192, 8192], P('ch', 'seq'), may hold values from -0.09375 to 0.09375
- grad_out: bfloat16 [2048, 8192], P('seq', 'ch'), may hold values from -6 to 6
Outputs:
- mixed: bfloat16 [2048, 8192], P('seq', 'ch')
- grad_query: bfloat16 [2048, 8192], P('seq', 'ch')
- grad_key: bfloat16 [2048, 8192], P('seq', 'ch')
- grad_value: bfloat16 [2048, 8192], P('seq', 'ch')
All inputs are finite; a program needn't handle non-finite values.
Results may differ from a plain program's by a relative error of at most 0.017.
Values may be sent and summed in bfloat16 or wider, within the bound.
A program may use at most 128 MiB of HBM per device.

v0:
```python
import math
import jax
import jax.numpy as jnp
from jax import lax
from jax.sharding import PartitionSpec as P


def from_behind(block, axis, distance):
    devices = range(lax.axis_size(axis))
    route = [(i - distance, i) for i in devices if i - distance in devices]
    return lax.ppermute(block, axis, route)


def entering(shard, axis, join, neutral, backward):
    count = lax.axis_size(axis)
    place = lax.axis_index(axis)
    ahead = count - 1 - place if backward else place
    gathered = jax.tree.map(
        lambda a, kind: lax.all_gather(a.astype(kind), axis), shard, (jnp.bfloat16, jnp.bfloat16)
    )
    state = jax.tree.map(lambda a, e: jnp.zeros_like(a) + jnp.asarray(e, a.dtype), shard, neutral)

    def one(turn, state):
        source = count - 1 - turn if backward else turn
        return join(
            state,
            jax.tree.map(
                lambda a, own: lax.dynamic_index_in_dim(a, source, 0, False).astype(own.dtype),
                gathered,
                shard,
            ),
        )

    return lax.fori_loop(0, ahead, one, state)


def chain_combine(earlier, later):
    return (earlier[0] * later[0], earlier[1] * later[0] + later[1])


def per_device(query, key, value, short_taps, decay_rate, residue, skip_gain, out_weight, grad_out):
    tok_rows, chan_width = query.shape
    tap_count = short_taps.shape[0]
    mode_count = decay_rate.shape[0]
    highest = lax.Precision.HIGHEST
    streams = jnp.stack([query, key, value])
    before = from_behind(streams[:, tok_rows - (tap_count - 1) :, :], "seq", 1)
    extended = jnp.concatenate([before, streams], axis=1).astype(jnp.float32)
    featured = jnp.zeros((3, tok_rows, chan_width), jnp.float32)
    for tap_index in range(tap_count):
        begin = tap_count - 1 - tap_index
        featured = (
            featured + short_taps[tap_index][:, None, :] * extended[:, begin : begin + tok_rows, :]
        )
    q_short = featured[0]
    k_short = featured[1]
    v_short = featured[2]
    gated = k_short * v_short
    columns = lax.all_gather(out_weight, "seq", axis=1, tiled=True)
    block_len = math.gcd(tok_rows, 128)
    block_count = tok_rows // block_len
    mode_scale = residue * jnp.sqrt(-jnp.expm1(-2.0 * decay_rate))
    offsets = jnp.arange(block_len).astype(jnp.float32)
    decay_pos = jnp.exp(-decay_rate[None, :, :] * offsets[:, None, None])
    filter_block = jnp.sum(mode_scale[None, :, :] * decay_pos, axis=1)
    filter_padded = jnp.concatenate(
        [jnp.zeros((block_len, chan_width), jnp.float32), filter_block], axis=0
    )
    lag_steps = jnp.arange(block_len)
    lag_index = block_len + lag_steps[:, None] - lag_steps[None, :]
    toeplitz = jnp.take(filter_padded, lag_index, axis=0)
    to_end = jnp.flip(decay_pos, 0)
    from_entry = mode_scale[None, :, :] * decay_pos * jnp.exp(-decay_rate)[None, :, :]
    step_decay = jnp.exp(-decay_rate * block_len)
    device_decay = jnp.exp(-decay_rate * tok_rows)
    block_steps = jnp.arange(block_count).astype(jnp.float32)
    block_decay = jnp.exp(-decay_rate[None, :, :] * block_len * block_steps[:, None, None])

    def local_pass(signal):
        blocks = signal.reshape(block_count, block_len, chan_width)
        intra = jnp.einsum("ijc,bjc->bic", toeplitz, blocks, precision=highest)
        ends = jnp.einsum("jnc,bjc->bnc", to_end, blocks, precision=highest)

        def advance(state, end_state):
            return (state * step_decay + end_state, state)

        final, entries = lax.scan(advance, jnp.zeros((mode_count, chan_width), jnp.float32), ends)
        return (intra, entries, final)

    def finish(intra, entries, entry_dev):
        starts = entries + block_decay * entry_dev[None, :, :]
        result = intra + jnp.einsum("inc,bnc->bic", from_entry, starts, precision=highest)
        return result.reshape(tok_rows, chan_width)

    def carried(final, later):
        identity = (jnp.ones_like(device_decay), jnp.zeros_like(final))
        if later:
            prefix = entering((device_decay, final), "seq", chain_combine, identity, True)
        else:
            prefix = entering((device_decay, final), "seq", chain_combine, identity, False)
        return prefix[1]

    intra, entries, final = local_pass(gated)
    entry_dev = carried(final, False)
    long_out = finish(intra, entries, entry_dev) + skip_gain[None, :] * gated
    mixer = (q_short * long_out).astype(jnp.bfloat16)
    partial_value = jnp.dot(mixer, columns, preferred_element_type=jnp.float32)
    mixed = lax.psum_scatter(
        partial_value.astype(jnp.bfloat16), "ch", scatter_dimension=1, tiled=True
    )
    grad_mixer = lax.dot_general(
        lax.all_gather(grad_out, "ch", axis=1, tiled=True),
        columns,
        (((1,), (1,)), ((), ())),
        preferred_element_type=jnp.float32,
    )
    grad_qshort = grad_mixer * long_out
    grad_long = grad_mixer * q_short
    intra_b, entries_b, final_b = local_pass(jnp.flip(grad_long, 0))
    exit_dev = carried(final_b, True)
    grad_gated = jnp.flip(finish(intra_b, entries_b, exit_dev), 0) + skip_gain[None, :] * grad_long
    grad_stack = jnp.stack([grad_qshort, grad_gated * v_short, grad_gated * k_short])
    after = from_behind(grad_stack[:, : tap_count - 1, :], "seq", -1)
    extended_back = jnp.concatenate([grad_stack, after], axis=1)
    grads = jnp.zeros((3, tok_rows, chan_width), jnp.float32)
    for tap_index in range(tap_count):
        grads = (
            grads
            + short_taps[tap_index][:, None, :]
            * extended_back[:, tap_index : tap_index + tok_rows, :]
        )
    grads = grads.astype(jnp.bfloat16)
    return (mixed, grads[0], grads[1], grads[2])


def solution(mesh):
    in_specs = (
        P("seq", "ch"),
        P("seq", "ch"),
        P("seq", "ch"),
        P(None, None, "ch"),
        P(None, "ch"),
        P(None, "ch"),
        P("ch"),
        P("ch", "seq"),
        P("seq", "ch"),
    )
    out_specs = (P("seq", "ch"), P("seq", "ch"), P("seq", "ch"), P("seq", "ch"))
    return jax.shard_map(
        per_device, mesh=mesh, in_specs=in_specs, out_specs=out_specs, check_vma=False
    )
```

profile of v0, /device:TPU:32, one launch (start us, length us, event | category | flops | bytes accessed | tf_op | source)
XLA Modules:
  0.0 294.9 jit_solution(6199740509660682278)
XLA Ops:
  7.2 0.0 all-gather.8.cloned.1.call-start
  7.2 0.7 all-gather.8.cloned.1.call-update
  7.9 0.0 all-gather.6.cloned.1.call-start
  7.9 0.7 all-gather.6.cloned.1.call-update
  8.6 0.0 reduce-scatter.2.cloned.1.call-start
  8.7 0.7 pad_maximum_fusion.2
  9.4 1.9 collective-permute-start
  11.4 0.7 slice_bitcast_fusion.6
  12.1 0.8 sqrt_multiply_fusion
  12.9 3.1 %multiply_exponential_fusion = (f32[128,16,512]{2,1,0:T(8,128)}, f32[128,512]{1,0:T(8,128)S(1)}) fusion(f32[128]{0:T(128)S(1)} %iota_convert_fusion, f32[16,512]{1,0:T(8,128)S(1)} %get-tuple-element.208, f32[16,512]{1,0:T(8,128)S(1)} %get-tuple-element.207), kind=kLoop, calls=%fused_computation.12 | loop fusion | flops 3080192 | bytes 4522496 | tf_op jit(solution)/shard_map/exp | solution.py:64
  16.0 0.1 fusion.10
  16.1 0.1 fusion.13
  16.3 0.0 copy-start
  16.3 0.0 copy-start.1
  16.3 0.0 copy-start.2
  16.3 64.1 %gather_fusion = f32[16384,512]{1,0:T(8,128)} fusion(f32[256,512]{1,0:T(8,128)S(1)} %concatenate.10, s32[16384]{0:T(1024)S(1)} %fusion.10), kind=kCustom, calls=%fused_computation | custom fusion | bytes 67174400 | tf_op jit(solution)/shard_map/jit(_take)/gather | solution.py:71
  80.5 0.0 collective-permute-done
  80.5 0.0 copy-done
  80.5 0.0 copy-done.1
  80.5 0.0 copy-done.2
  80.5 0.1 maximum_convert_fusion
  80.6 0.2 fusion.3
  80.9 0.0 all-gather.8.cloned.1.call-done
  80.9 40.2 %all-gather.6.cloned.1.call-done = bf16[512,8192]{1,0:T(8,128)(2,1)} async-done(((bf16[512,512]{1,0:T(8,128)(2,1)}), bf16[512,8192]{1,0:T(8,128)(2,1)}) %all-gather.6.cloned.1.call-update) | async-done | bytes 8388624 | tf_op jit(solution)/shard_map/all_gather | solution.py:59
  121.1 6.9 %fusion.8 = (f32[128,512]{1,0:T(8,128)S(1)}, f32[128,512]{1,0:T(8,128)S(1)}) fusion(f32[3,128,512]{2,1,0:T(8,128)S(1)} %fusion.3, bf16[128,8192]{1,0:T(8,128)(2,1)} %all-gather.8.cloned.1.call-done, bf16[512,8192]{1,0:T(8,128)(2,1)} %all-gather.6.cloned.1.call-done), kind=kOutput, calls=%fused_computation.40 | convolution fusion | flops 1073807360 | bytes 11272192 | tf_op jit(solution)/shard_map/dot_general | solution.py:111
  128.1 0.0 copy-start.3
  128.1 0.1 rev.12
  128.2 3.1 %multiply_reduce_fusion.3 = (f32[512,16]{0,1:T(8,128)S(1)}, f32[512,16]{0,1:T(8,128)S(1)}) fusion(f32[128,16,512]{2,1,0:T(8,128)} %get-tuple-element.199, f32[512,128]{0,1:T(8,128)S(1)} %bitcast.129, f32[512,128]{0,1:T(8,128)S(1)} %multiply_bitcast_fusion.1), kind=kLoop, calls=%fused_computation.9 | loop fusion | flops 4177920 | bytes 4784128 | tf_op jit(solution)/shard_map/jnc,bjc->bnc/dot_general | solution.py:82
  131.3 0.0 copy-done.3
  131.3 17.1 %all-gather = bf16[256,512]{1,0:T(8,128)(2,1)S(1)} all-gather(bf16[16,512]{1,0:T(8,128)(2,1)S(1)} %get-tuple-element.205), channel_id=2, replica_groups=mesh['seq'=16,'ch'=16] {'seq'}, dimensions={0}, use_global_device_ids=true | all-gather | bytes 278528 | tf_op jit(solution)/shard_map/all_gather | solution.py:19
  148.5 16.2 %all-gather.2 = bf16[256,512]{1,0:T(8,128)(2,1)S(1)} all-gather(bf16[16,512]{1,0:T(8,128)(2,1)S(1)} %get-tuple-element.206), channel_id=4, replica_groups=mesh['seq'=16,'ch'=16] {'seq'}, dimensions={0}, use_global_device_ids=true | all-gather | bytes 278528 | tf_op jit(solution)/shard_map/all_gather | solution.py:19
  164.7 0.6 while.17
  165.3 15.6 %all-gather.1 = bf16[256,512]{1,0:T(8,128)(2,1)S(1)} all-gather(bf16[16,512]{1,0:T(8,128)(2,1)S(1)} %get-tuple-element.204), channel_id=3, replica_groups=mesh['seq'=16,'ch'=16] {'seq'}, dimensions={0}, use_global_device_ids=true | all-gather | bytes 278528 | tf_op jit(solution)/shard_map/all_gather | solution.py:19
  180.8 0.2 while.16
  181.1 0.0 copy-start.4
  181.1 18.0 %multiply_reduce_fusion = (f32[512,128]{0,1:T(8,128)S(1)}, f32[512,128]{0,1:T(8,128)S(1)}) fusion(f32[128,128,512]{2,1,0:T(8,128)} %bitcast.128, f32[512,128]{0,1:T(8,128)S(1)} %bitcast.130, pred[128,128]{1,0:T(8,128)(4,1)S(1)} %fusion.13, f32[512,128]{0,1:T(8,128)S(1)} %multiply_bitcast_fusion.1), kind=kLoop, calls=%fused_computation.5 | loop fusion | flops 41811968 | bytes 34619392 | tf_op jit(solution)/shard_map/ijc,bjc->bic/dot_general | solution.py:81
  199.1 2.5 multiply_reduce_fusion.2
  201.7 0.1 rev.13
  201.8 0.2 fusion.6
  202.1 6.0 %convolution_convert_fusion = bf16[128,8192]{1,0:T(8,128)(2,1)} fusion(bf16[512,8192]{1,0:T(8,128)(2,1)} %all-gather.6.cloned.1.call-done, f32[128,512]{1,0:T(8,128)S(1)} %get-tuple-element.195, f32[3,128,512]{2,1,0:T(8,128)S(1)} %fusion.3), kind=kOutput, calls=%fused_computation.7 | convolution fusion | flops 1074921472 | bytes 11010048 | tf_op jit(solution)/shard_map/dot_general | solution.py:107
  208.0 0.0 reduce-scatter.2.cloned.1.call-update
  208.1 0.1 pad_maximum_fusion.1
  208.1 3.4 %collective-permute-start.1 = (f32[3,2,512]{2,1,0:T(2,128)S(1)}, f32[3,2,512]{2,1,0:T(2,128)S(1)}, u32[]{:S(2)}, u32[]{:S(2)}) collective-permute-start(f32[3,2,512]{2,1,0:T(2,128)S(1)} %slice.75), channel_id=1, source_target_pairs={{16,0},{32,16},{48,32},{64,48},{80,64},{96,80},{112,96},{128,112},... | collective-permute-start | bytes 36872 | tf_op jit(solution)/shard_map/ppermute | solution.py:11
  211.5 1.4 collective-permute-done.1
  212.9 0.1 pad_maximum_fusion
  213.0 0.3 fusion.1
  213.2 0.8 slice_bitcast_fusion.1
  214.0 74.4 %reduce-scatter.2.cloned.1.call-done = bf16[128,512]{1,0:T(8,128)(2,1)} async-done(((bf16[128,8192]{1,0:T(8,128)(2,1)}), bf16[128,512]{1,0:T(8,128)(2,1)}) %reduce-scatter.2.cloned.1.call-update) | async-done | bytes 131088 | tf_op jit(solution)/shard_map/reduce_scatter | solution.py:108
  (26 shorter events, 0.4 us)
Async XLA Ops:
  7.2 73.7 %all-gather.8.cloned.1.call-start = ((), (), s32[]{:S(2)}) async-start(), calls=%async_computation.3 | async-start | bytes 2228224 | tf_op jit(solution)/shard_map/all_gather | solution.py:112
  7.9 113.2 %all-gather.6.cloned.1.call-start = ((), (), s32[]{:S(2)}) async-start(), calls=%async_computation.1 | async-start | bytes 8912896 | tf_op jit(solution)/shard_map/all_gather | solution.py:59
  8.6 279.7 %reduce-scatter.2.cloned.1.call-start = ((), (), s32[]{:S(2)}) async-start(), calls=%async_computation.2 | async-start | bytes 2228224 | tf_op jit(solution)/shard_map/reduce_scatter | solution.py:108
  9.4 71.0 %collective-permute-start = (bf16[3,2,512]{2,1,0:T(2,128)(2,1)S(1)}, bf16[3,2,512]{2,1,0:T(2,128)(2,1)S(1)}, u32[]{:S(2)}, u32[]{:S(2)}) collective-permute-start(bf16[3,2,512]{2,1,0:T(2,128)(2,1)S(1)} %pad_maximum_fusion.2), channel_id=1, source_target_pairs={{0,16},{16,32},{32,48},{48,64},{64,80},{80,96},{96,112},{112,128},... | collective-permute-start | bytes 18440 | tf_op jit(solution)/shard_map/ppermute | solution.py:11
  16.3 64.2 %copy-start = (bf16[128,512]{1,0:T(8,128)(2,1)S(1)}, bf16[128,512]{1,0:T(8,128)(2,1)}, u32[]{:S(2)}) copy-start(bf16[128,512]{1,0:T(8,128)(2,1)} %param.15) | copy-start | bytes 393220
  16.3 64.2 %copy-start.1 = (bf16[128,512]{1,0:T(8,128)(2,1)S(1)}, bf16[128,512]{1,0:T(8,128)(2,1)}, u32[]{:S(2)}) copy-start(bf16[128,512]{1,0:T(8,128)(2,1)} %param.14) | copy-start | bytes 393220
  16.3 64.2 %copy-start.2 = (bf16[128,512]{1,0:T(8,128)(2,1)S(1)}, bf16[128,512]{1,0:T(8,128)(2,1)}, u32[]{:S(2)}) copy-start(bf16[128,512]{1,0:T(8,128)(2,1)} %param.13) | copy-start | bytes 393220
  128.1 3.2 %copy-start.3 = (f32[16,512]{1,0:T(8,128)S(1)}, f32[16,512]{1,0:T(8,128)}, u32[]{:S(2)}) copy-start(f32[16,512]{1,0:T(8,128)} %param.17) | copy-start | bytes 98308
  181.1 20.7 %copy-start.4 = (f32[512]{0:T(512)S(1)}, f32[512]{0:T(512)}, u32[]{:S(2)}) copy-start(f32[512]{0:T(512)} %param.19) | copy-start | bytes 6148
  208.1 4.7 %collective-permute-start.1 = (f32[3,2,512]{2,1,0:T(2,128)S(1)}, f32[3,2,512]{2,1,0:T(2,128)S(1)}, u32[]{:S(2)}, u32[]{:S(2)}) collective-permute-start(f32[3,2,512]{2,1,0:T(2,128)S(1)} %slice.75), channel_id=1, source_target_pairs={{16,0},{32,16},{48,32},{64,48},{80,64},{96,80},{112,96},{128,112},... | collective-permute-start | bytes 36872 | tf_op jit(solution)/shard_map/ppermute | solution.py:11
Sparse Core Ops, SparseCore 0:
  10.4 55.2 all-gather.7
  67.6 53.5 all-gather.5
  208.2 80.1 reduce-scatter.1
where the time goes:
time: 295 us
  waiting for transfers between devices  117 us (40%)
  local copies, waits for them, and re-layouts  66 us (22%)
  blocking collectives  48.9 us (17%)
  other arithmetic  29.7 us (10%)
  between operations  14 us (5%)
  matrix products  12.9 us (4%)
  starting transfers between devices  5.38 us (2%)
    reduce_scatter x1, waiting for transfers between devices, per_device(): lax.psum_scatter(partial_value.astype(jnp.bfloat16), 'ch', scatter_dimens...  74.4 us
    gather x1, local copies, waits for them, and re-layouts, per_device(): toeplitz = jnp.take(filter_padded, lag_index, axis=0)  64.1 us
    all_gather x3, blocking collectives, entering(): lax.all_gather(a.astype(kind), axis)  48.9 us
    all_gather x1, waiting for transfers between devices, per_device(): columns = lax.all_gather(out_weight, 'seq', axis=1, tiled=True)  40.2 us
    dot_general x1, other arithmetic, local_pass(): intra = jnp.einsum('ijc,bjc->bic', toeplitz, blocks, precision=highest)  18 us
    dot_general x1, matrix products, per_device(): lax.dot_general(lax.all_gather(grad_out, 'ch', axis=1, tiled=True), colum...  6.94 us
    dot_general x1, matrix products, per_device(): partial_value = jnp.dot(mixer, columns, preferred_element_type=jnp.float32)  5.99 us
  transfers between devices with their start and end apart: 5, of which 3 were waited for; matrix products, arithmetic and copies ran while one was open for 24% of the time, Pallas kernels for 0%

commit v1 on v0

--- a/solution.py
+++ b/solution.py
@@ -56,7 +56,9 @@
     k_short = featured[1]
     v_short = featured[2]
     gated = k_short * v_short
-    columns = lax.all_gather(out_weight, "seq", axis=1, tiled=True)
+    columns = jnp.concatenate(
+        lax.all_to_all(jnp.stack([out_weight] * lax.axis_size("seq")), "seq", 0, 0), axis=1
+    )
     block_len = math.gcd(tok_rows, 128)
     block_count = tok_rows // block_len
     mode_scale = residue * jnp.sqrt(-jnp.expm1(-2.0 * decay_rate))

time: 295 us -> 378 us (1.28)
  waiting for transfers between devices: 117 us -> 188 us
  starting transfers between devices: 5.38 us -> 14.4 us
  local copies, waits for them, and re-layouts: 66 us -> 70.7 us
    ppermute x2, waiting for transfers between devices: 1.39 us -> 112 us  [from_behind(): return lax.ppermute(block, axis, route)]
    all_gather x1 -> x0, waiting for transfers between devices: 40.2 us -> none  [per_device(): columns = lax.all_gather(out_weight, 'seq', axis=1, tiled=True)]
    all_to_all x0 -> x1, starting transfers between devices: none -> 8.73 us  [per_device(): lax.all_to_all(jnp.stack([out_weight] * lax.axis_size('seq')), 'seq', 0, 0)]
    another operation x0 -> x1, local copies, waits for them, and re-layouts: none -> 4.01 us  [per_device(): jnp.stack([out_weight] * lax.axis_size('seq'))]
  transfers between devices with their start and end apart: 5 -> 5, of which waited for: 3 -> 4; matrix products, arithmetic and copies ran while one was open for 24% -> 18% of each run, Pallas kernels for 0% -> 0%
where the time goes in v1:
time: 378 us; the launch traced here: 377 us
  waiting for transfers between devices  188 us (50%)
  local copies, waits for them, and re-layouts  70.7 us (19%)
  blocking collectives  48.6 us (13%)
  other arithmetic  28.3 us (7%)
  starting transfers between devices  14.4 us (4%)
  between operations  14.4 us (4%)
  matrix products  12.8 us (3%)
    ppermute x2, waiting for transfers between devices, from_behind(): return lax.ppermute(block, axis, route)  112 us
    reduce_scatter x1, waiting for transfers between devices, per_device(): lax.psum_scatter(partial_value.astype(jnp.bfloat16), 'ch', scatter_dimens...  74.2 us
    gather x1, local copies, waits for them, and re-layouts, per_device(): toeplitz = jnp.take(filter_padded, lag_index, axis=0)  64.3 us
    all_gather x3, blocking collectives, entering(): lax.all_gather(a.astype(kind), axis)  48.6 us
    dot_general x1, other arithmetic, local_pass(): intra = jnp.einsum('ijc,bjc->bic', toeplitz, blocks, precision=highest)  18 us
    all_to_all x1, starting transfers between devices, per_device(): lax.all_to_all(jnp.stack([out_weight] * lax.axis_size('seq')), 'seq', 0, 0)  8.73 us
  transfers between devices with their start and end apart: 5, of which 4 were waited for; matrix products, arithmetic and copies ran while one was open for 18% of the time, Pallas kernels for 0%

profile of v1, /device:TPU:32, one launch (start us, length us, event | category | flops | bytes accessed | tf_op | source)
XLA Modules:
  0.0 377.2 jit_solution(14537823993215702368)
XLA Ops:
  7.2 1.3 copy.14
  8.4 4.0 %stack.22 = bf16[16,512,512]{1,2,0:T(8,128)(2,1)} broadcast(bf16[512,512]{0,1:T(8,128)(2,1)S(1)} %copy.14), dimensions={1,2} | broadcast | bytes 8912896 | tf_op jit(solution)/shard_map/stack | solution.py:60
  12.4 0.0 copy-start
  12.4 0.0 copy-start.3
  12.5 0.0 copy-start.5
  12.5 8.7 %all-to-all-start = ((bf16[16,512,512]{1,2,0:T(8,128)(2,1)}), bf16[16,512,512]{1,2,0:T(8,128)(2,1)}, u32[]{:S(2)}, u32[]{:S(2)}) async-start(bf16[16,512,512]{1,2,0:T(8,128)(2,1)} %stack.22), calls=%async_computation | async-start | bytes 16777216 | tf_op jit(solution)/shard_map/all_to_all | solution.py:60
  21.2 0.0 all-gather.5.cloned.1.call-start
  21.2 0.7 all-gather.5.cloned.1.call-update
  21.9 0.0 reduce-scatter.2.cloned.1.call-start
  22.0 0.0 copy-done
  22.0 0.0 copy-done.1
  22.0 0.0 copy-done.2
  22.0 2.1 collective-permute-start
  24.1 0.0 copy-done.6
  24.1 0.0 copy-done.3
  24.1 0.0 copy-done.5
  24.2 3.2 multiply_exponential_fusion
  27.4 0.1 fusion.18
  27.5 0.1 fusion.21
  27.7 64.3 %gather_fusion = f32[16384,512]{1,0:T(8,128)} fusion(f32[256,512]{1,0:T(8,128)S(1)} %concatenate.10, s32[16384]{0:T(1024)S(1)} %fusion.18), kind=kCustom, calls=%fused_computation | custom fusion | bytes 67174400 | tf_op jit(solution)/shard_map/jit(_take)/gather | solution.py:73
  91.9 110.9 %collective-permute-done = bf16[3,2,512]{2,1,0:T(2,128)(2,1)S(1)} collective-permute-done((bf16[3,2,512]{2,1,0:T(2,128)(2,1)S(1)}, bf16[3,2,512]{2,1,0:T(2,128)(2,1)S(1)}, u32[]{:S(2)}, u32[]{:S(2)}) %collective-permute-start) | collective-permute-done | bytes 6176 | tf_op jit(solution)/shard_map/ppermute | solution.py:11
  202.8 0.1 maximum_convert_fusion
  202.9 0.2 fusion.3
  203.2 0.0 all-gather.5.cloned.1.call-done
  203.3 0.4 all-to-all-done
  203.6 5.3 %bitcast_multiply_fusion = (f32[128,512]{1,0:T(8,128)S(1)}, f32[128,512]{1,0:T(8,128)S(1)}) fusion(f32[3,128,512]{2,1,0:T(8,128)S(1)} %fusion.3, bf16[128,8192]{1,0:T(8,128)(2,1)} %all-gather.5.cloned.1.call-done, bf16[512,8192]{0,1:T(8,128)(2,1)} %bitcast.36), kind=kOutput, calls=%fused_computation.30 | convolution fusion | flops 1073807360 | bytes 11272192 | tf_op jit(solution)/shard_map/dot_general | solution.py:113
  208.9 0.1 rev.12
  209.0 3.1 multiply_reduce_fusion.3
  212.1 16.8 %all-gather = bf16[256,512]{1,0:T(8,128)(2,1)S(1)} all-gather(bf16[16,512]{1,0:T(8,128)(2,1)S(1)} %get-tuple-element.202), channel_id=2, replica_groups=mesh['seq'=16,'ch'=16] {'seq'}, dimensions={0}, use_global_device_ids=true | all-gather | bytes 278528 | tf_op jit(solution)/shard_map/all_gather | solution.py:19
  229.0 16.4 %all-gather.2 = bf16[256,512]{1,0:T(8,128)(2,1)S(1)} all-gather(bf16[16,512]{1,0:T(8,128)(2,1)S(1)} %get-tuple-element.203), channel_id=4, replica_groups=mesh['seq'=16,'ch'=16] {'seq'}, dimensions={0}, use_global_device_ids=true | all-gather | bytes 278528 | tf_op jit(solution)/shard_map/all_gather | solution.py:19
  245.4 0.6 while.17
  245.9 15.4 %all-gather.1 = bf16[256,512]{1,0:T(8,128)(2,1)S(1)} all-gather(bf16[16,512]{1,0:T(8,128)(2,1)S(1)} %get-tuple-element.201), channel_id=3, replica_groups=mesh['seq'=16,'ch'=16] {'seq'}, dimensions={0}, use_global_device_ids=true | all-gather | bytes 278528 | tf_op jit(solution)/shard_map/all_gather | solution.py:19
  261.4 0.2 while.16
  261.6 0.0 copy-start.4
  261.6 18.0 %multiply_reduce_fusion = (f32[512,128]{0,1:T(8,128)S(1)}, f32[512,128]{0,1:T(8,128)S(1)}) fusion(f32[128,128,512]{2,1,0:T(8,128)} %bitcast.138, f32[512,128]{0,1:T(8,128)S(1)} %bitcast.140, pred[128,128]{1,0:T(8,128)(4,1)S(1)} %fusion.21, f32[512,128]{0,1:T(8,128)S(1)} %fusion.16), kind=kLoop, calls=%fused_computation.5 | loop fusion | flops 41811968 | bytes 34619392 | tf_op jit(solution)/shard_map/ijc,bjc->bic/dot_general | solution.py:83
  279.6 2.5 multiply_reduce_fusion.2
  282.2 0.0 copy-done.4
  282.2 7.5 %convolution_convert_fusion = bf16[128,8192]{1,0:T(8,128)(2,1)} fusion(bf16[512,8192]{0,1:T(8,128)(2,1)} %bitcast.36, f32[3,128,512]{2,1,0:T(8,128)S(1)} %fusion.3, f32[512]{0:T(512)S(1)} %copy-done.4, f32[512,128]{0,1:T(8,128)S(1)} %get-tuple-element.165, f32[512,128]{0,1:T(8,128)S(1)} %get-tuple-element.169), kind=kOutput, calls=%fused_computation.7 | convolution fusion | flops 1075183616 | bytes 11798528 | tf_op jit(solution)/shard_map/dot_general | solution.py:109
  289.7 0.0 reduce-scatter.2.cloned.1.call-update
  289.7 0.1 rev.13
  289.9 0.2 fusion.8
  290.1 0.1 pad_maximum_fusion.1
  290.2 3.5 collective-permute-start.1
  293.7 1.4 collective-permute-done.1
  295.1 0.1 pad_maximum_fusion
  295.1 0.3 fusion.1
  295.4 0.8 slice_bitcast_fusion
  296.2 74.2 %reduce-scatter.2.cloned.1.call-done = bf16[128,512]{1,0:T(8,128)(2,1)} async-done(((bf16[128,8192]{1,0:T(8,128)(2,1)}), bf16[128,512]{1,0:T(8,128)(2,1)}) %reduce-scatter.2.cloned.1.call-update) | async-done | bytes 131088 | tf_op jit(solution)/shard_map/reduce_scatter | solution.py:110
  (31 shorter events, 0.4 us)
Async XLA Ops:
  12.4 9.5 %copy-start = (bf16[128,512]{1,0:T(8,128)(2,1)S(1)}, bf16[128,512]{1,0:T(8,128)(2,1)}, u32[]{:S(2)}) copy-start(bf16[128,512]{1,0:T(8,128)(2,1)} %param.15) | copy-start | bytes 393220
  12.4 9.6 %copy-start.1 = (bf16[128,512]{1,0:T(8,128)(2,1)S(1)}, bf16[128,512]{1,0:T(8,128)(2,1)}, u32[]{:S(2)}) copy-start(bf16[128,512]{1,0:T(8,128)(2,1)} %param.14) | copy-start | bytes 393220
  12.4 9.6 %copy-start.2 = (bf16[128,512]{1,0:T(8,128)(2,1)S(1)}, bf16[128,512]{1,0:T(8,128)(2,1)}, u32[]{:S(2)}) copy-start(bf16[128,512]{1,0:T(8,128)(2,1)} %param.13) | copy-start | bytes 393220
  12.4 11.7 %copy-start.6 = (f32[3,3,512]{2,1,0:T(4,128)S(1)}, f32[3,3,512]{2,1,0:T(4,128)}, u32[]{:S(2)}) copy-start(f32[3,3,512]{2,1,0:T(4,128)} %param.16) | copy-start | bytes 55300
  12.4 11.7 %copy-start.3 = (f32[16,512]{1,0:T(8,128)S(1)}, f32[16,512]{1,0:T(8,128)}, u32[]{:S(2)}) copy-start(f32[16,512]{1,0:T(8,128)} %param.17) | copy-start | bytes 98308
  12.5 11.7 %copy-start.5 = (f32[16,512]{1,0:T(8,128)S(1)}, f32[16,512]{1,0:T(8,128)}, u32[]{:S(2)}) copy-start(f32[16,512]{1,0:T(8,128)} %param.18) | copy-start | bytes 98308
  12.5 191.1 %all-to-all-start = ((bf16[16,512,512]{1,2,0:T(8,128)(2,1)}), bf16[16,512,512]{1,2,0:T(8,128)(2,1)}, u32[]{:S(2)}, u32[]{:S(2)}) async-start(bf16[16,512,512]{1,2,0:T(8,128)(2,1)} %stack.22), calls=%async_computation | async-start | bytes 16777216 | tf_op jit(solution)/shard_map/all_to_all | solution.py:60
  21.2 182.0 %all-gather.5.cloned.1.call-start = ((), (), s32[]{:S(2)}) async-start(), calls=%async_computation.3 | async-start | bytes 2228224 | tf_op jit(solution)/shard_map/all_gather | solution.py:114
  21.9 348.4 %reduce-scatter.2.cloned.1.call-start = ((), (), s32[]{:S(2)}) async-start(), calls=%async_computation.2 | async-start | bytes 2228224 | tf_op jit(solution)/shard_map/reduce_scatter | solution.py:110
  22.0 180.8 %collective-permute-start = (bf16[3,2,512]{2,1,0:T(2,128)(2,1)S(1)}, bf16[3,2,512]{2,1,0:T(2,128)(2,1)S(1)}, u32[]{:S(2)}, u32[]{:S(2)}) collective-permute-start(bf16[3,2,512]{2,1,0:T(2,128)(2,1)S(1)} %pad_maximum_fusion.2), channel_id=1, source_target_pairs={{0,16},{16,32},{32,48},{48,64},{64,80},{80,96},{96,112},{112,128},... | collective-permute-start | bytes 18440 | tf_op jit(solution)/shard_map/ppermute | solution.py:11
  261.6 20.5 %copy-start.4 = (f32[512]{0:T(512)S(1)}, f32[512]{0:T(512)}, u32[]{:S(2)}) copy-start(f32[512]{0:T(512)} %param.19) | copy-start | bytes 6148
  290.2 4.9 %collective-permute-start.1 = (f32[3,2,512]{2,1,0:T(2,128)S(1)}, f32[3,2,512]{2,1,0:T(2,128)S(1)}, u32[]{:S(2)}, u32[]{:S(2)}) collective-permute-start(f32[3,2,512]{2,1,0:T(2,128)S(1)} %slice.75), channel_id=1, source_target_pairs={{16,0},{32,16},{48,32},{64,48},{80,64},{96,80},{112,96},{128,112},... | collective-permute-start | bytes 36872 | tf_op jit(solution)/shard_map/ppermute | solution.py:11
Sparse Core Ops, SparseCore 0:
  24.4 53.8 all-gather.4
  289.8 80.4 reduce-scatter.1
